TPU v7x, 32 devices: a whole 2x2x4 slice. The times are simulated.
32 devices in a mesh: leaf: 4 (over z), row: 2 (over x), top: 4 (over y, core).
Axes of the slice: x: 2, y: 2, z: 4, core: 2. Of those that a mesh axis runs over, the one named last changes fastest.
Arguments:
- loads: bfloat16 [4, 2, 4, 1, 256, 32], P('leaf', 'row', 'top'), may hold values from -6 to 6
- flux_maps: bfloat16 [4, 2, 4, 640, 256], P('leaf', 'row', 'top'), may hold values from -0.375 to 0.375
- chain_maps: float32 [4, 2, 4, 640, 640], P('leaf', 'row', 'top')
- leaf_maps: bfloat16 [4, 2, 4, 1, 256, 256], P('leaf', 'row', 'top'), may hold values from -0.375 to 0.375
- edge_maps: bfloat16 [4, 2, 4, 1, 256, 640], P('leaf', 'row', 'top'), may hold values from -0.25 to 0.25
- top_maps: bfloat16 [4, 2, 4, 1, 256, 128], P('leaf', 'row', 'top'), may hold values from -0.5 to 0.5
- slot_nodes: int32 [4, 2, 4, 128], P('leaf', 'row', 'top'), may hold values from 0 to 8191
- slot_counts: int32 [4, 2, 4], P('leaf', 'row', 'top'), may hold values from 1 to 128, 320 in all within a row
- top_loads: float32 [8192, 32], P('leaf'), may hold values from -6 to 6
- top_inverse: float32 [8192, 8192], P('top', ('leaf', 'row')), may hold values from -0.0625 to 0.0625
Outputs:
- solution: bfloat16 [4, 2, 4, 1, 256, 32], P('leaf', 'row', 'top')
- top_values: float32 [8192, 32], P('top')
Inputs may be any that keep to these rules, and one draw needn't show every extreme that they name: `slot_counts`: over the 4 subtrees of one x-y cell (same x and y, all t) the live slots sum to 320, and one of those subtrees has all 128 slots live.
All inputs are finite; a program needn't handle non-finite values. No bound on the sum of `slot_counts` on one device may be relied on, other than what follows from the above.
Results may differ from a plain program's by a relative error of at most 0.0046.
Values sent between devices are 32-bit elements; how exact they have to be, the bound alone decides.
A program may use at most 64 MiB of HBM per device.

v0:
```python
import jax
import jax.numpy as jnp
from jax import lax
from jax.sharding import PartitionSpec as P


def passed_along(value, axis, steps):
    count = lax.axis_size(axis)
    first, last = (max(0, -steps), min(count, count - steps))
    return lax.ppermute(value, axis, [(source, source + steps) for source in range(first, last)])


def body(
    loads,
    flux_maps,
    chain_maps,
    leaf_maps,
    edge_maps,
    top_maps,
    slot_nodes,
    slot_counts,
    top_loads,
    top_inverse,
):
    leaf_count = loads.shape[3]
    node_count = loads.shape[4]
    rhs_count = loads.shape[5]
    sep_width = chain_maps.shape[-1]
    slot_total = slot_nodes.shape[-1]
    largest_level = lax.Precision.HIGHEST
    local_loads = loads.reshape(leaf_count, node_count, rhs_count)
    flattened = loads.reshape(leaf_count * node_count, rhs_count)
    fluxes = jnp.dot(
        flux_maps.reshape(sep_width, leaf_count * node_count),
        flattened,
        preferred_element_type=jnp.float32,
    )
    combine_operator = chain_maps.reshape(sep_width, sep_width)
    chain_index = lax.axis_index("leaf")

    def advance(step_index, carried):
        earlier = passed_along(carried, "leaf", 1)
        advanced = (
            jnp.dot(
                combine_operator,
                earlier,
                precision=largest_level,
                preferred_element_type=jnp.float32,
            )
            + fluxes
        )
        return jnp.where(chain_index == step_index, advanced, carried)

    states = lax.fori_loop(1, lax.axis_size("leaf"), advance, fluxes)
    slot_ids = slot_nodes.reshape(slot_total)
    is_live = lax.iota(jnp.int32, slot_total) < slot_counts.reshape(())
    chosen_entries = jnp.where(is_live[:, None], states[:slot_total], jnp.float32(0.0))
    block_rows = top_loads.shape[0]
    row_ids = lax.iota(jnp.int32, block_rows * lax.axis_size("leaf"))
    match_table = (row_ids[:, None] == slot_ids[None, :]).astype(jnp.float32)
    top_block = lax.psum_scatter(
        jnp.dot(
            match_table, chosen_entries, precision=largest_level, preferred_element_type=jnp.float32
        ),
        "leaf",
        scatter_dimension=0,
        tiled=True,
    )
    top_block = lax.psum(top_block, ("row", "top"))
    rhs_block = top_loads - top_block
    column_rows = top_inverse.shape[1]
    rhs_piece = lax.dynamic_slice_in_dim(
        rhs_block, lax.axis_index("row") * column_rows, column_rows, 0
    )
    partial_value = jnp.dot(
        top_inverse, rhs_piece, precision=largest_level, preferred_element_type=jnp.float32
    )
    owned_rows = lax.psum(partial_value, ("leaf", "row"))
    shard_piece = lax.all_gather(owned_rows, "top", axis=0, tiled=True)
    row_ids = lax.iota(jnp.int32, shard_piece.shape[0])
    match_table = ((slot_ids[:, None] == row_ids[None, :]) & is_live[:, None]).astype(jnp.float32)
    boundary = jnp.dot(
        match_table, shard_piece, precision=largest_level, preferred_element_type=jnp.float32
    )
    states_low = states.astype(jnp.bfloat16)
    boundary_low = boundary.astype(jnp.bfloat16)
    summed = jnp.einsum(
        "lij,ljr->lir",
        leaf_maps.reshape(leaf_count, node_count, node_count),
        local_loads,
        preferred_element_type=jnp.float32,
    )
    summed = summed + jnp.einsum(
        "lik,kr->lir",
        edge_maps.reshape(leaf_count, node_count, sep_width),
        states_low,
        preferred_element_type=jnp.float32,
    )
    summed = summed + jnp.einsum(
        "lic,cr->lir",
        top_maps.reshape(leaf_count, node_count, slot_total),
        boundary_low,
        preferred_element_type=jnp.float32,
    )
    solution = summed.astype(jnp.bfloat16).reshape(1, 1, 1, leaf_count, node_count, rhs_count)
    return (solution, owned_rows)


def solution(mesh):
    in_specs = (
        P("leaf", "row", "top", None, None, None),
        P("leaf", "row", "top", None, None),
        P("leaf", "row", "top", None, None),
        P("leaf", "row", "top", None, None, None),
        P("leaf", "row", "top", None, None, None),
        P("leaf", "row", "top", None, None, None),
        P("leaf", "row", "top", None),
        P("leaf", "row", "top"),
        P("leaf", None),
        P("top", ("leaf", "row")),
    )
    out_specs = (P("leaf", "row", "top", None, None, None), P("top", None))
    return jax.shard_map(body, mesh=mesh, in_specs=in_specs, out_specs=out_specs, check_vma=False)
```

profile of v0, /device:TPU:0, one launch (start us, length us, event | category | flops | bytes accessed | tf_op | source)
XLA Modules:
  0.0 237.6 jit_solution(16142841711911786712)
XLA Ops:
  7.2 0.0 copy-start
  7.2 0.0 reduce-scatter.2.cloned.1.call-start
  7.9 0.2 copy-done
  8.2 0.9 fusion.15
  9.1 0.0 copy-start.7
  9.1 0.0 copy-start.4
  9.1 29.0 %while.13 = (s32[]{:T(128)}, f32[640,32]{0,1:T(8,128)S(1)}, s32[]{:T(128)}, f32[640,640]{1,0:T(8,128)}, f32[640,32]{0,1:T(8,128)S(1)}, /*index=5*/s32[]{:T(128)}) while((s32[]{:T(128)}, f32[640,32]{0,1:T(8,128)S(1)}, s32[]{:T(128)}, f32[640,640]{1,0:T(8,128)}, f32[640,32]{0,1:T(8,128)S(1)}, /*index=5*/s32[]{:T(128)}) %tuple.44), condition=%wide.region_1.2_spmd, body=%wide.region_0.1_spmd.sunk | while | flops 157327360 | bytes 2293879 | solution.py:54
  9.1 5.1 %collective-permute-start = (f32[640,32]{0,1:T(8,128)S(1)}, f32[640,32]{0,1:T(8,128)S(1)}, u32[]{:S(2)}, u32[]{:S(2)}) collective-permute-start(f32[640,32]{0,1:T(8,128)S(1)} %get-tuple-element.145), channel_id=1, source_target_pairs={{0,8},{8,16},{16,24},{1,9},{9,17},{17,25},{2,10},{10,18},{18,26},{... | collective-permute-start | bytes 245768 | tf_op jit(solution)/shard_map/while/body/eval_jaxpr/ppermute | solution.py:10
  14.2 2.0 collective-permute-done
  16.3 3.1 %fusion.39 = f32[640,32]{0,1:T(8,128)S(1)} fusion(f32[640,32]{0,1:T(8,128)S(1)} %get-tuple-element.145, f32[640,32]{0,1:T(8,128)S(1)} %get-tuple-element.154, f32[640,640]{1,0:T(8,128)} %get-tuple-element.153, f32[640,32]{0,1:T(8,128)S(1)} %collective-permute-done, pred[]{:T(512)S(6)} %eq.69), kind=kOutput, calls=%fused_computation.1.clone.1 | convolution fusion | flops 157327360 | bytes 1966081 | tf_op jit(solution)/shard_map/while/body/eval_jaxpr/dot_general | solution.py:44
  19.4 4.3 %collective-permute-start = (f32[640,32]{0,1:T(8,128)S(1)}, f32[640,32]{0,1:T(8,128)S(1)}, u32[]{:S(2)}, u32[]{:S(2)}) collective-permute-start(f32[640,32]{0,1:T(8,128)S(1)} %get-tuple-element.145), channel_id=1, source_target_pairs={{0,8},{8,16},{16,24},{1,9},{9,17},{17,25},{2,10},{10,18},{18,26},{... | collective-permute-start | bytes 245768 | tf_op jit(solution)/shard_map/while/body/eval_jaxpr/ppermute | solution.py:10
  23.7 2.0 collective-permute-done
  25.7 3.1 %fusion.39 = f32[640,32]{0,1:T(8,128)S(1)} fusion(f32[640,32]{0,1:T(8,128)S(1)} %get-tuple-element.145, f32[640,32]{0,1:T(8,128)S(1)} %get-tuple-element.154, f32[640,640]{1,0:T(8,128)} %get-tuple-element.153, f32[640,32]{0,1:T(8,128)S(1)} %collective-permute-done, pred[]{:T(512)S(6)} %eq.69), kind=kOutput, calls=%fused_computation.1.clone.1 | convolution fusion | flops 157327360 | bytes 1966081 | tf_op jit(solution)/shard_map/while/body/eval_jaxpr/dot_general | solution.py:44
  28.8 4.3 %collective-permute-start = (f32[640,32]{0,1:T(8,128)S(1)}, f32[640,32]{0,1:T(8,128)S(1)}, u32[]{:S(2)}, u32[]{:S(2)}) collective-permute-start(f32[640,32]{0,1:T(8,128)S(1)} %get-tuple-element.145), channel_id=1, source_target_pairs={{0,8},{8,16},{16,24},{1,9},{9,17},{17,25},{2,10},{10,18},{18,26},{... | collective-permute-start | bytes 245768 | tf_op jit(solution)/shard_map/while/body/eval_jaxpr/ppermute | solution.py:10
  33.1 2.0 collective-permute-done
  35.1 3.1 %fusion.39 = f32[640,32]{0,1:T(8,128)S(1)} fusion(f32[640,32]{0,1:T(8,128)S(1)} %get-tuple-element.145, f32[640,32]{0,1:T(8,128)S(1)} %get-tuple-element.154, f32[640,640]{1,0:T(8,128)} %get-tuple-element.153, f32[640,32]{0,1:T(8,128)S(1)} %collective-permute-done, pred[]{:T(512)S(6)} %eq.69), kind=kOutput, calls=%fused_computation.1.clone.1 | convolution fusion | flops 157327360 | bytes 1966081 | tf_op jit(solution)/shard_map/while/body/eval_jaxpr/dot_general | solution.py:44
  38.2 0.0 copy-done.7
  38.2 3.3 %fusion.2 = f32[8192,32]{0,1:T(8,128)} fusion(s32[128]{0:T(128)S(1)} %bitcast.45, f32[640,32]{0,1:T(8,128)S(1)} %get-tuple-element.96, pred[128]{0:T(512)(128)(4,1)S(1)} %iota_compare_fusion.3), kind=kOutput, calls=%fused_computation.5 | convolution fusion | flops 403705856 | bytes 1065984 | tf_op jit(solution)/shard_map/dot_general | solution.py:62
  41.5 0.0 reduce-scatter.2.cloned.1.call-update
  41.5 0.0 all-reduce.3.cloned.1.call-start
  41.6 29.4 %reduce-scatter.2.cloned.1.call-done = f32[2048,32]{0,1:T(8,128)} async-done(((f32[8192,32]{0,1:T(8,128)}), f32[2048,32]{0,1:T(8,128)}) %reduce-scatter.2.cloned.1.call-update) | async-done | bytes 262160 | tf_op jit(solution)/shard_map/reduce_scatter | solution.py:61
  71.0 0.0 all-reduce.3.cloned.1.call-update
  71.0 0.0 all-reduce.5.cloned.1.call-start
  71.1 0.0 copy-start.2
  71.1 0.0 copy-start.3
  71.1 0.0 copy-start.6
  71.1 55.4 %all-reduce.3.cloned.1.call-done = f32[2048,32]{0,1:T(8,128)} async-done(((f32[2048,32]{0,1:T(8,128)}), f32[2048,32]{0,1:T(8,128)}) %all-reduce.3.cloned.1.call-update) | async-done | bytes 262160 | tf_op jit(solution)/shard_map/psum | solution.py:69
  126.5 0.0 copy-done.4
  126.5 11.7 %convolution_bitcast_fusion = f32[2048,32]{0,1:T(8,128)} fusion(f32[2048,1024]{1,0:T(8,128)} %param.21, f32[2048,32]{0,1:T(8,128)} %all-reduce.3.cloned.1.call-done, s32[]{:T(128)S(6)} %select_n.24, f32[2048,32]{0,1:T(8,128)S(1)} %copy-done.4), kind=kOutput, calls=%fused_computation.7 | convolution fusion | flops 805339136 | bytes 8912900 | tf_op jit(solution)/shard_map/dot_general | solution.py:75
  138.2 0.0 copy-start.5
  138.2 0.0 all-reduce.5.cloned.1.call-update
  138.2 0.0 all-gather.2.cloned.1.call-start
  138.2 70.5 %all-reduce.5.cloned.1.call-done = f32[2048,32]{0,1:T(8,128)} async-done(((f32[2048,32]{0,1:T(8,128)}), f32[2048,32]{0,1:T(8,128)}) %all-reduce.5.cloned.1.call-update) | async-done | bytes 262160 | tf_op jit(solution)/shard_map/psum | solution.py:78
  208.7 0.0 copy-start.1
  208.7 0.0 all-gather.2.cloned.1.call-update
  208.8 0.0 copy-done.2
  208.8 0.2 convolution_bitcast_fusion.2
  208.9 0.0 copy-done.3
  209.0 0.0 copy-done.6
  209.0 0.2 convolution_add_fusion.1
  209.2 16.9 %all-gather.2.cloned.1.call-done = f32[8192,32]{0,1:T(8,128)} async-done(((f32[2048,32]{0,1:T(8,128)}), f32[8192,32]{0,1:T(8,128)}) %all-gather.2.cloned.1.call-update) | async-done | bytes 1048592 | tf_op jit(solution)/shard_map/all_gather | solution.py:79
  226.1 3.5 %fusion.8 = bf16[128,32]{1,0:T(8,128)(2,1)S(1)} fusion(f32[8192,32]{0,1:T(8,128)} %all-gather.2.cloned.1.call-done, s32[128]{0:T(128)S(1)} %bitcast.46, pred[128]{0:T(512)(128)(4,1)S(1)} %iota_compare_fusion.3), kind=kOutput, calls=%fused_computation.11 | convolution fusion | flops 404754432 | bytes 1057408 | tf_op jit(solution)/shard_map/dot_general | solution.py:82
  229.6 0.0 copy-done.5
  229.6 0.8 fusion.13
  230.4 0.0 copy-done.1
  230.4 0.7 copy.21
  (2 shorter events, 0.0 us)
Async XLA Ops:
  7.2 1.0 copy-start
  7.2 63.8 %reduce-scatter.2.cloned.1.call-start = ((), (), s32[]{:S(2)}) async-start(), calls=%async_computation.1 | async-start | bytes 1310720 | tf_op jit(solution)/shard_map/reduce_scatter | solution.py:61
  9.1 29.1 %copy-start.7 = (s32[1,1,1,128]{3,2,1,0:T(1,128)S(1)}, s32[1,1,1,128]{3,2,1,0:T(1,128)}, u32[]{:S(2)}) copy-start(s32[1,1,1,128]{3,2,1,0:T(1,128)} %param.18) | copy-start | bytes 1540
  9.1 117.4 %copy-start.4 = (f32[2048,32]{0,1:T(8,128)S(1)}, f32[2048,32]{0,1:T(8,128)}, u32[]{:S(2)}) copy-start(f32[2048,32]{0,1:T(8,128)} %param.20) | copy-start | bytes 786436
  9.1 7.1 %collective-permute-start = (f32[640,32]{0,1:T(8,128)S(1)}, f32[640,32]{0,1:T(8,128)S(1)}, u32[]{:S(2)}, u32[]{:S(2)}) collective-permute-start(f32[640,32]{0,1:T(8,128)S(1)} %get-tuple-element.145), channel_id=1, source_target_pairs={{0,8},{8,16},{16,24},{1,9},{9,17},{17,25},{2,10},{10,18},{18,26},{... | collective-permute-start | bytes 245768 | tf_op jit(solution)/shard_map/while/body/eval_jaxpr/ppermute | solution.py:10
  19.4 6.3 %collective-permute-start = (f32[640,32]{0,1:T(8,128)S(1)}, f32[640,32]{0,1:T(8,128)S(1)}, u32[]{:S(2)}, u32[]{:S(2)}) collective-permute-start(f32[640,32]{0,1:T(8,128)S(1)} %get-tuple-element.145), channel_id=1, source_target_pairs={{0,8},{8,16},{16,24},{1,9},{9,17},{17,25},{2,10},{10,18},{18,26},{... | collective-permute-start | bytes 245768 | tf_op jit(solution)/shard_map/while/body/eval_jaxpr/ppermute | solution.py:10
  28.8 6.3 %collective-permute-start = (f32[640,32]{0,1:T(8,128)S(1)}, f32[640,32]{0,1:T(8,128)S(1)}, u32[]{:S(2)}, u32[]{:S(2)}) collective-permute-start(f32[640,32]{0,1:T(8,128)S(1)} %get-tuple-element.145), channel_id=1, source_target_pairs={{0,8},{8,16},{16,24},{1,9},{9,17},{17,25},{2,10},{10,18},{18,26},{... | collective-permute-start | bytes 245768 | tf_op jit(solution)/shard_map/while/body/eval_jaxpr/ppermute | solution.py:10
  41.5 84.9 %all-reduce.3.cloned.1.call-start = ((), (), s32[]{:S(2)}) async-start(), calls=%async_computation.2 | async-start | bytes 524288 | tf_op jit(solution)/shard_map/psum | solution.py:69
  71.0 137.7 %all-reduce.5.cloned.1.call-start = ((), (), s32[]{:S(2)}) async-start(), calls=%async_computation.3 | async-start | bytes 524288 | tf_op jit(solution)/shard_map/psum | solution.py:78
  71.1 137.7 %copy-start.2 = (bf16[1,1,1,1,256,640]{5,4,3,2,1,0:T(8,128)(2,1)S(1)}, bf16[1,1,1,1,256,640]{5,4,3,2,1,0:T(8,128)(2,1)}, u32[]{:S(2)}) copy-start(bf16[1,1,1,1,256,640]{5,4,3,2,1,0:T(8,128)(2,1)} %param.16) | copy-start | bytes 983044
  71.1 137.9 %copy-start.3 = (bf16[1,1,1,1,256,256]{5,4,3,2,1,0:T(8,128)(2,1)S(1)}, bf16[1,1,1,1,256,256]{5,4,3,2,1,0:T(8,128)(2,1)}, u32[]{:S(2)}) copy-start(bf16[1,1,1,1,256,256]{5,4,3,2,1,0:T(8,128)(2,1)} %param.15) | copy-start | bytes 393220
  71.1 137.9 %copy-start.6 = (bf16[1,1,1,1,256,32]{4,5,3,2,1,0:T(8,128)(2,1)S(1)}, bf16[1,1,1,1,256,32]{4,5,3,2,1,0:T(8,128)(2,1)}, u32[]{:S(2)}) copy-start(bf16[1,1,1,1,256,32]{4,5,3,2,1,0:T(8,128)(2,1)} %param.12) | copy-start | bytes 49156
  138.2 91.4 %copy-start.5 = (bf16[1,1,1,1,256,128]{5,4,3,2,1,0:T(8,128)(2,1)S(1)}, bf16[1,1,1,1,256,128]{5,4,3,2,1,0:T(8,128)(2,1)}, u32[]{:S(2)}) copy-start(bf16[1,1,1,1,256,128]{5,4,3,2,1,0:T(8,128)(2,1)} %param.17) | copy-start | bytes 196612
  138.2 87.9 %all-gather.2.cloned.1.call-start = ((), (), s32[]{:S(2)}) async-start(), calls=%async_computation.4 | async-start | bytes 1310720 | tf_op jit(solution)/shard_map/all_gather | solution.py:79
  208.7 21.6 %copy-start.1 = (f32[2048,32]{0,1:T(8,128)S(1)}, f32[2048,32]{0,1:T(8,128)}, u32[]{:S(2)}) copy-start(f32[2048,32]{0,1:T(8,128)} %all-reduce.5.cloned.1.call-done) | copy-start | bytes 786436
Sparse Core Ops, SparseCore 0:
  41.6 29.3 reduce-scatter.1
  74.1 52.3 all-reduce.2
  138.3 70.3 all-reduce.4
  210.2 15.8 all-gather.1
where the time goes:
time: 238 us
  waiting for transfers between devices  178 us (75%)
  matrix products  29.7 us (12%)
  between operations  14.6 us (6%)
  starting transfers between devices  13.8 us (6%)
    psum x1, waiting for transfers between devices, body(): owned_rows = lax.psum(partial_value, ('leaf', 'row'))  70.5 us
    psum x1, waiting for transfers between devices, body(): top_block = lax.psum(top_block, ('row', 'top'))  55.4 us
    reduce_scatter x1, waiting for transfers between devices, body(): lax.psum_scatter(jnp.dot(match_table, chosen_entries, precision=largest_l...  29.4 us
    all_gather x1, waiting for transfers between devices, body(): shard_piece = lax.all_gather(owned_rows, 'top', axis=0, tiled=True)  16.9 us
    ppermute x3, starting transfers between devices, passed_along(): lax.ppermute(value, axis, [(source, source + steps) for source in range(f...  13.7 us
    dot_general x1, matrix products, body(): jnp.dot(top_inverse, rhs_piece, precision=largest_level, preferred_elemen...  11.7 us
    dot_general x3, matrix products, advance(): jnp.dot(combine_operator, earlier, precision=largest_level, preferred_ele...  9.17 us
    ppermute x3, waiting for transfers between devices, passed_along(): lax.ppermute(value, axis, [(source, source + steps) for source in range(f...  6.09 us
  transfers between devices with their start and end apart: 7, of which 7 were waited for; matrix products, arithmetic and copies ran while one was open for 0% of the time, Pallas kernels for 0%

commit v1 on v0

--- a/solution.py
+++ b/solution.py
@@ -66,7 +66,7 @@
         scatter_dimension=0,
         tiled=True,
     )
-    top_block = lax.psum(top_block, ("row", "top"))
+    top_block = jnp.sum(lax.all_gather(top_block, ("row", "top")), axis=0)
     rhs_block = top_loads - top_block
     column_rows = top_inverse.shape[1]
     rhs_piece = lax.dynamic_slice_in_dim(

time: 238 us -> 214 us (0.90)
  waiting for transfers between devices: 178 us -> 152 us
  local copies, waits for them, and re-layouts: 1.05 us -> 3.85 us
    psum x1 -> x0, waiting for transfers between devices: 55.4 us -> none  [body(): top_block = lax.psum(top_block, ('row', 'top'))]
    all_gather x0 -> x1, waiting for transfers between devices: none -> 28.1 us  [body(): top_block = jnp.sum(lax.all_gather(top_block, ('row', 'top')), axis=0)]
    unnamed x18 -> x19, local copies, waits for them, and re-layouts: 1.05 us -> 3.85 us
where the time goes in v1:
time: 214 us; the launch traced here: 213 us
  waiting for transfers between devices  152 us (71%)
  matrix products  28.6 us (13%)
  between operations  14.6 us (7%)
  starting transfers between devices  13.7 us (6%)
  local copies, waits for them, and re-layouts  3.85 us (2%)
    psum x1, waiting for transfers between devices, body(): owned_rows = lax.psum(partial_value, ('leaf', 'row'))  71.1 us
    reduce_scatter x1, waiting for transfers between devices, body(): lax.psum_scatter(jnp.dot(match_table, chosen_entries, precision=largest_l...  29.5 us
    all_gather x1, waiting for transfers between devices, body(): top_block = jnp.sum(lax.all_gather(top_block, ('row', 'top')), axis=0)  28.1 us
    all_gather x1, waiting for transfers between devices, body(): shard_piece = lax.all_gather(owned_rows, 'top', axis=0, tiled=True)  16.9 us
    ppermute x3, starting transfers between devices, passed_along(): lax.ppermute(value, axis, [(source, source + steps) for source in range(f...  13.5 us
    dot_general x1, matrix products, body(): jnp.dot(top_inverse, rhs_piece, precision=largest_level, preferred_elemen...  10.6 us
    dot_general x3, matrix products, advance(): jnp.dot(combine_operator, earlier, precision=largest_level, preferred_ele...  9.17 us
    ppermute x3, waiting for transfers between devices, passed_along(): lax.ppermute(value, axis, [(source, source + steps) for source in range(f...  6.09 us
  transfers between devices with their start and end apart: 7, of which 7 were waited for; matrix products, arithmetic and copies ran while one was open for 0% of the time, Pallas kernels for 0%

profile of v1, /device:TPU:0, one launch (start us, length us, event | category | flops | bytes accessed | tf_op | source)
XLA Modules:
  0.0 213.2 jit_solution(3093330935586319221)
XLA Ops:
  7.2 0.0 copy-start
  7.2 0.0 reduce-scatter.2.cloned.1.call-start
  7.9 0.2 copy-done
  8.2 0.9 fusion.15
  9.1 0.0 copy-start.7
  9.1 28.9 %while.13 = (s32[]{:T(128)}, f32[640,32]{0,1:T(8,128)S(1)}, s32[]{:T(128)}, f32[640,640]{1,0:T(8,128)}, f32[640,32]{0,1:T(8,128)S(1)}, /*index=5*/s32[]{:T(128)}) while((s32[]{:T(128)}, f32[640,32]{0,1:T(8,128)S(1)}, s32[]{:T(128)}, f32[640,640]{1,0:T(8,128)}, f32[640,32]{0,1:T(8,128)S(1)}, /*index=5*/s32[]{:T(128)}) %tuple.44), condition=%wide.region_1.2_spmd, body=%wide.region_0.1_spmd.sunk | while | flops 157327360 | bytes 2293879 | solution.py:54
  9.1 5.0 %collective-permute-start = (f32[640,32]{0,1:T(8,128)S(1)}, f32[640,32]{0,1:T(8,128)S(1)}, u32[]{:S(2)}, u32[]{:S(2)}) collective-permute-start(f32[640,32]{0,1:T(8,128)S(1)} %get-tuple-element.145), channel_id=1, source_target_pairs={{0,8},{8,16},{16,24},{1,9},{9,17},{17,25},{2,10},{10,18},{18,26},{... | collective-permute-start | bytes 245768 | tf_op jit(solution)/shard_map/while/body/eval_jaxpr/ppermute | solution.py:10
  14.1 2.0 collective-permute-done
  16.1 3.1 %fusion.39 = f32[640,32]{0,1:T(8,128)S(1)} fusion(f32[640,32]{0,1:T(8,128)S(1)} %get-tuple-element.145, f32[640,32]{0,1:T(8,128)S(1)} %get-tuple-element.154, f32[640,640]{1,0:T(8,128)} %get-tuple-element.153, f32[640,32]{0,1:T(8,128)S(1)} %collective-permute-done, pred[]{:T(512)S(6)} %eq.69), kind=kOutput, calls=%fused_computation.1.clone.1 | convolution fusion | flops 157327360 | bytes 1966081 | tf_op jit(solution)/shard_map/while/body/eval_jaxpr/dot_general | solution.py:44
  19.2 4.3 %collective-permute-start = (f32[640,32]{0,1:T(8,128)S(1)}, f32[640,32]{0,1:T(8,128)S(1)}, u32[]{:S(2)}, u32[]{:S(2)}) collective-permute-start(f32[640,32]{0,1:T(8,128)S(1)} %get-tuple-element.145), channel_id=1, source_target_pairs={{0,8},{8,16},{16,24},{1,9},{9,17},{17,25},{2,10},{10,18},{18,26},{... | collective-permute-start | bytes 245768 | tf_op jit(solution)/shard_map/while/body/eval_jaxpr/ppermute | solution.py:10
  23.5 2.0 collective-permute-done
  25.5 3.1 %fusion.39 = f32[640,32]{0,1:T(8,128)S(1)} fusion(f32[640,32]{0,1:T(8,128)S(1)} %get-tuple-element.145, f32[640,32]{0,1:T(8,128)S(1)} %get-tuple-element.154, f32[640,640]{1,0:T(8,128)} %get-tuple-element.153, f32[640,32]{0,1:T(8,128)S(1)} %collective-permute-done, pred[]{:T(512)S(6)} %eq.69), kind=kOutput, calls=%fused_computation.1.clone.1 | convolution fusion | flops 157327360 | bytes 1966081 | tf_op jit(solution)/shard_map/while/body/eval_jaxpr/dot_general | solution.py:44
  28.6 4.3 %collective-permute-start = (f32[640,32]{0,1:T(8,128)S(1)}, f32[640,32]{0,1:T(8,128)S(1)}, u32[]{:S(2)}, u32[]{:S(2)}) collective-permute-start(f32[640,32]{0,1:T(8,128)S(1)} %get-tuple-element.145), channel_id=1, source_target_pairs={{0,8},{8,16},{16,24},{1,9},{9,17},{17,25},{2,10},{10,18},{18,26},{... | collective-permute-start | bytes 245768 | tf_op jit(solution)/shard_map/while/body/eval_jaxpr/ppermute | solution.py:10
  32.9 2.0 collective-permute-done
  35.0 3.1 %fusion.39 = f32[640,32]{0,1:T(8,128)S(1)} fusion(f32[640,32]{0,1:T(8,128)S(1)} %get-tuple-element.145, f32[640,32]{0,1:T(8,128)S(1)} %get-tuple-element.154, f32[640,640]{1,0:T(8,128)} %get-tuple-element.153, f32[640,32]{0,1:T(8,128)S(1)} %collective-permute-done, pred[]{:T(512)S(6)} %eq.69), kind=kOutput, calls=%fused_computation.1.clone.1 | convolution fusion | flops 157327360 | bytes 1966081 | tf_op jit(solution)/shard_map/while/body/eval_jaxpr/dot_general | solution.py:44
  38.0 0.0 copy-done.7
  38.0 3.3 %fusion.2 = f32[8192,32]{0,1:T(8,128)} fusion(s32[128]{0:T(128)S(1)} %bitcast.51, f32[640,32]{0,1:T(8,128)S(1)} %get-tuple-element.96, pred[128]{0:T(512)(128)(4,1)S(1)} %iota_compare_fusion.3), kind=kOutput, calls=%fused_computation.5 | convolution fusion | flops 403705856 | bytes 1065984 | tf_op jit(solution)/shard_map/dot_general | solution.py:62
  41.3 0.0 copy-start.4
  41.3 0.0 reduce-scatter.2.cloned.1.call-update
  41.4 0.0 all-gather.6.cloned.1.call-start
  41.4 29.5 %reduce-scatter.2.cloned.1.call-done = f32[2048,32]{0,1:T(8,128)} async-done(((f32[8192,32]{0,1:T(8,128)}), f32[2048,32]{0,1:T(8,128)}) %reduce-scatter.2.cloned.1.call-update) | async-done | bytes 262160 | tf_op jit(solution)/shard_map/reduce_scatter | solution.py:61
  70.9 0.0 all-gather.6.cloned.1.call-update
  70.9 0.0 all-reduce.2.cloned.1.call-start
  71.0 28.1 %all-gather.6.cloned.1.call-done = f32[16384,32]{0,1:T(8,128)} async-done(((f32[2048,32]{0,1:T(8,128)}), f32[16384,32]{0,1:T(8,128)}) %all-gather.6.cloned.1.call-update) | async-done | bytes 2097168 | tf_op jit(solution)/shard_map/all_gather | solution.py:69
  99.1 2.8 %copy.12 = f32[4,8,8,2048]{3,2,1,0:T(8,128)S(1)} copy(f32[4,8,8,2048]{3,1,2,0:T(8,128)} %bitcast.50) | data formatting | bytes 4194304
  101.9 0.5 bitcast_reduce_fusion
  102.5 0.0 copy-done.4
  102.5 0.0 copy-start.2
  102.5 0.0 copy-start.3
  102.5 0.0 copy-start.6
  102.5 10.6 %convolution_bitcast_fusion = f32[2048,32]{0,1:T(8,128)} fusion(f32[2048,1024]{1,0:T(8,128)} %param.21, f32[2048,32]{0,1:T(8,128)S(1)} %bitcast_reduce_fusion, s32[]{:T(128)S(6)} %select_n.24, f32[2048,32]{0,1:T(8,128)S(1)} %copy-done.4), kind=kOutput, calls=%fused_computation.7 | convolution fusion | flops 805339136 | bytes 8912900 | tf_op jit(solution)/shard_map/dot_general | solution.py:75
  113.1 0.0 copy-start.5
  113.1 0.0 all-reduce.2.cloned.1.call-update
  113.2 0.0 all-gather.4.cloned.1.call-start
  113.2 71.1 %all-reduce.2.cloned.1.call-done = f32[2048,32]{0,1:T(8,128)} async-done(((f32[2048,32]{0,1:T(8,128)}), f32[2048,32]{0,1:T(8,128)}) %all-reduce.2.cloned.1.call-update) | async-done | bytes 262160 | tf_op jit(solution)/shard_map/psum | solution.py:78
  184.3 0.0 copy-start.1
  184.3 0.0 all-gather.4.cloned.1.call-update
  184.4 0.0 copy-done.2
  184.4 0.2 convolution_bitcast_fusion.2
  184.5 0.0 copy-done.3
  184.6 0.0 copy-done.6
  184.6 0.2 convolution_add_fusion.1
  184.7 16.9 %all-gather.4.cloned.1.call-done = f32[8192,32]{0,1:T(8,128)} async-done(((f32[2048,32]{0,1:T(8,128)}), f32[8192,32]{0,1:T(8,128)}) %all-gather.4.cloned.1.call-update) | async-done | bytes 1048592 | tf_op jit(solution)/shard_map/all_gather | solution.py:79
  201.7 3.5 %fusion.8 = bf16[128,32]{1,0:T(8,128)(2,1)S(1)} fusion(f32[8192,32]{0,1:T(8,128)} %all-gather.4.cloned.1.call-done, s32[128]{0:T(128)S(1)} %bitcast.52, pred[128]{0:T(512)(128)(4,1)S(1)} %iota_compare_fusion.3), kind=kOutput, calls=%fused_computation.12 | convolution fusion | flops 404754432 | bytes 1057408 | tf_op jit(solution)/shard_map/dot_general | solution.py:82
  205.2 0.0 copy-done.5
  205.2 0.8 fusion.13
  205.9 0.0 copy-done.1
  205.9 0.7 copy.21
  (2 shorter events, 0.0 us)
Async XLA Ops:
  7.2 1.0 copy-start
  7.2 63.7 %reduce-scatter.2.cloned.1.call-start = ((), (), s32[]{:S(2)}) async-start(), calls=%async_computation.1 | async-start | bytes 1310720 | tf_op jit(solution)/shard_map/reduce_scatter | solution.py:61
  9.1 28.9 %copy-start.7 = (s32[1,1,1,128]{3,2,1,0:T(1,128)S(1)}, s32[1,1,1,128]{3,2,1,0:T(1,128)}, u32[]{:S(2)}) copy-start(s32[1,1,1,128]{3,2,1,0:T(1,128)} %param.18) | copy-start | bytes 1540
  9.1 7.0 %collective-permute-start = (f32[640,32]{0,1:T(8,128)S(1)}, f32[640,32]{0,1:T(8,128)S(1)}, u32[]{:S(2)}, u32[]{:S(2)}) collective-permute-start(f32[640,32]{0,1:T(8,128)S(1)} %get-tuple-element.145), channel_id=1, source_target_pairs={{0,8},{8,16},{16,24},{1,9},{9,17},{17,25},{2,10},{10,18},{18,26},{... | collective-permute-start | bytes 245768 | tf_op jit(solution)/shard_map/while/body/eval_jaxpr/ppermute | solution.py:10
  19.2 6.3 %collective-permute-start = (f32[640,32]{0,1:T(8,128)S(1)}, f32[640,32]{0,1:T(8,128)S(1)}, u32[]{:S(2)}, u32[]{:S(2)}) collective-permute-start(f32[640,32]{0,1:T(8,128)S(1)} %get-tuple-element.145), channel_id=1, source_target_pairs={{0,8},{8,16},{16,24},{1,9},{9,17},{17,25},{2,10},{10,18},{18,26},{... | collective-permute-start | bytes 245768 | tf_op jit(solution)/shard_map/while/body/eval_jaxpr/ppermute | solution.py:10
  28.6 6.3 %collective-permute-start = (f32[640,32]{0,1:T(8,128)S(1)}, f32[640,32]{0,1:T(8,128)S(1)}, u32[]{:S(2)}, u32[]{:S(2)}) collective-permute-start(f32[640,32]{0,1:T(8,128)S(1)} %get-tuple-element.145), channel_id=1, source_target_pairs={{0,8},{8,16},{16,24},{1,9},{9,17},{17,25},{2,10},{10,18},{18,26},{... | collective-permute-start | bytes 245768 | tf_op jit(solution)/shard_map/while/body/eval_jaxpr/ppermute | solution.py:10
  41.3 61.1 %copy-start.4 = (f32[2048,32]{0,1:T(8,128)S(1)}, f32[2048,32]{0,1:T(8,128)}, u32[]{:S(2)}) copy-start(f32[2048,32]{0,1:T(8,128)} %param.20) | copy-start | bytes 786436
  41.4 57.7 %all-gather.6.cloned.1.call-start = ((), (), s32[]{:S(2)}) async-start(), calls=%async_computation.4 | async-start | bytes 2359296 | tf_op jit(solution)/shard_map/all_gather | solution.py:69
  70.9 113.4 %all-reduce.2.cloned.1.call-start = ((), (), s32[]{:S(2)}) async-start(), calls=%async_computation.2 | async-start | bytes 524288 | tf_op jit(solution)/shard_map/psum | solution.py:78
  102.5 81.9 %copy-start.2 = (bf16[1,1,1,1,256,640]{5,4,3,2,1,0:T(8,128)(2,1)S(1)}, bf16[1,1,1,1,256,640]{5,4,3,2,1,0:T(8,128)(2,1)}, u32[]{:S(2)}) copy-start(bf16[1,1,1,1,256,640]{5,4,3,2,1,0:T(8,128)(2,1)} %param.16) | copy-start | bytes 983044
  102.5 82.1 %copy-start.3 = (bf16[1,1,1,1,256,256]{5,4,3,2,1,0:T(8,128)(2,1)S(1)}, bf16[1,1,1,1,256,256]{5,4,3,2,1,0:T(8,128)(2,1)}, u32[]{:S(2)}) copy-start(bf16[1,1,1,1,256,256]{5,4,3,2,1,0:T(8,128)(2,1)} %param.15) | copy-start | bytes 393220
  102.5 82.1 %copy-start.6 = (bf16[1,1,1,1,256,32]{4,5,3,2,1,0:T(8,128)(2,1)S(1)}, bf16[1,1,1,1,256,32]{4,5,3,2,1,0:T(8,128)(2,1)}, u32[]{:S(2)}) copy-start(bf16[1,1,1,1,256,32]{4,5,3,2,1,0:T(8,128)(2,1)} %param.12) | copy-start | bytes 49156
  113.1 92.0 %copy-start.5 = (bf16[1,1,1,1,256,128]{5,4,3,2,1,0:T(8,128)(2,1)S(1)}, bf16[1,1,1,1,256,128]{5,4,3,2,1,0:T(8,128)(2,1)}, u32[]{:S(2)}) copy-start(bf16[1,1,1,1,256,128]{5,4,3,2,1,0:T(8,128)(2,1)} %param.17) | copy-start | bytes 196612
  113.2 88.5 %all-gather.4.cloned.1.call-start = ((), (), s32[]{:S(2)}) async-start(), calls=%async_computation.3 | async-start | bytes 1310720 | tf_op jit(solution)/shard_map/all_gather | solution.py:79
  184.3 21.6 %copy-start.1 = (f32[2048,32]{0,1:T(8,128)S(1)}, f32[2048,32]{0,1:T(8,128)}, u32[]{:S(2)}) copy-start(f32[2048,32]{0,1:T(8,128)} %all-reduce.2.cloned.1.call-done) | copy-start | bytes 786436
Sparse Core Ops, SparseCore 0:
  41.5 29.3 reduce-scatter.1
  72.8 26.2 all-gather.5
  113.3 71.0 all-reduce.1
  185.7 15.8 all-gather.3
